TPU v7x, 32 devices: a whole 2x2x4 slice. The times are simulated.
32 devices in a mesh: rep: 2 (over y), sample: 4 (over z), head: 4 (over x, core).
Axes of the slice: x: 2, y: 2, z: 4, core: 2. Of those that a mesh axis runs over, the one named last changes fastest.
Arguments:
- x_pre: bfloat16 [8, 128, 8192], P(('rep', 'sample'), None, 'head'), parts along dimension 0, may hold values from -120 to 120
- z_pre: bfloat16 [8, 128, 8192], P(('rep', 'sample'), None, 'head'), parts along dimension 0, may hold values from -6 to 6
- b_pre: bfloat16 [8, 128, 512], P(('rep', 'sample')), parts along dimension 0, may hold values from -1.796875 to 1.796875
- c_pre: bfloat16 [8, 128, 512], P(('rep', 'sample')), parts along dimension 0, may hold values from -0.5390625 to 0.5390625
- dt_pre: float32 [8, 128, 128], P(('rep', 'sample'), None, 'head'), parts along dimension 0, may hold values from -1.5 to 7.5
- lengths: int32 [8], P(('rep', 'sample')), parts along dimension 0, may hold values from 64 to 128, as said below
- init_state: float32 [8, 128, 8192], P(('rep', 'sample'), None, 'head'), parts along dimension 0, may hold values from -6 to 6
- a_rates: float32 [128], P('head'), may hold values from 0.005 to 0.3
- dt_bias: float32 [128], P('head'), may hold values from -2 to -1
- skip_scale: float32 [128], P('head'), may hold values from 0.5 to 2
- norm_gain: float32 [8192], P('head'), may hold values from 0.5 to 1.5
- x_dec: bfloat16 [8, 4, 8192], P(('rep', 'sample'), None, 'head'), parts along dimension 0, may hold values from -120 to 120
- z_dec: bfloat16 [8, 4, 8192], P(('rep', 'sample'), None, 'head'), parts along dimension 0, may hold values from -6 to 6
- b_dec: bfloat16 [8, 4, 512], P(('rep', 'sample')), parts along dimension 0, may hold values from -6 to 6
- c_dec: bfloat16 [8, 4, 512], P(('rep', 'sample')), parts along dimension 0, may hold values from -0.5390625 to 0.5390625
- dt_dec: float32 [8, 4, 128], P(('rep', 'sample'), None, 'head'), parts along dimension 0, may hold values from -3 to 3
Outputs:
- out_pre: bfloat16 [8, 128, 8192], P(('rep', 'sample'), None, 'head'), parts along dimension 0
- final_state: bfloat16 [8, 128, 8192], P(('rep', 'sample'), None, 'head'), parts along dimension 0
- out_dec: bfloat16 [8, 4, 8192], P(('rep', 'sample'), None, 'head'), parts along dimension 0
There are 2 independent parts, one for each index of `rep`. A program takes and returns all parts, laid end to end along the dimension named above; an argument that names none is the same for every part. Nothing has to cross between parts.
Inputs may be any that keep to these rules, and one draw needn't show every extreme that they name: Each prompt's valid tokens are the first lengths[p] of its 128 positions; some prompt uses all 128.
All inputs are finite; a program needn't handle non-finite values.
Results may differ from a plain program's by a relative error of at most 0.006.
Values may be sent and summed in bfloat16 or wider, within the bound.
No kernel may reach another device: no remote copies, remote signals or barrier semaphores. Data moves between devices by JAX's collectives and lax.ppermute only.
A program may use at most 64 MiB of HBM per device.

v0:
```python
import jax
import jax.numpy as jnp
from jax import lax
from jax.sharding import PartitionSpec as P

H = 128
P_SIZE = 64
G = 4
BLOCK = 128
epsilon = 1e-05
highest = lax.Precision.HIGHEST


def group_owners(first_head, head_count):
    head_ids = first_head + jnp.arange(head_count, dtype=jnp.int32)
    return head_ids // (H // G)


def group_pick(owners):
    return (owners[:, None] == jnp.arange(G, dtype=jnp.int32)[None, :]).astype(jnp.float32)


def scan_prompt(inputs, b_rows, c_rows, step_delta, rates, skip_gain, start_state, owners):
    length = inputs.shape[0]
    head_count = step_delta.shape[1]
    head_width = inputs.shape[1] // head_count
    states = b_rows.shape[1] // G
    blocks = length // BLOCK
    b_groups = b_rows.reshape(blocks, BLOCK, G, states)
    c_groups = c_rows.reshape(blocks, BLOCK, G, states)
    group_scores = jnp.einsum(
        "cign,cjgn->cijg", c_groups, b_groups, preferred_element_type=jnp.float32
    )
    head_scores = jnp.take(group_scores, owners, axis=3)
    b_head = jnp.take(b_groups, owners, axis=2).astype(jnp.float32)
    c_head = jnp.take(c_groups, owners, axis=2).astype(jnp.float32)
    values = inputs.astype(jnp.float32).reshape(blocks, BLOCK, head_count, head_width)
    block_delta = step_delta.reshape(blocks, BLOCK, head_count)
    decays = jnp.cumsum(-block_delta * rates, axis=1)
    causal_mask = (jnp.arange(BLOCK)[:, None] >= jnp.arange(BLOCK)[None, :])[None, :, :, None]
    spread = decays[:, :, None, :] - decays[:, None, :, :]
    weights = jnp.where(causal_mask, jnp.exp(jnp.where(causal_mask, spread, 0.0)), 0.0)
    scores = head_scores * weights * block_delta[:, None, :, :]
    inner_part = jnp.einsum("cijh,cjhp->cihp", scores, values, precision=highest)
    tail_decay = jnp.exp(decays[:, -1:, :] - decays) * block_delta
    block_states = jnp.einsum(
        "cjhn,cjhp->cnhp", b_head * tail_decay[..., None], values, precision=highest
    )
    block_totals = jnp.exp(decays[:, -1, :])

    def carry_step(carried, pieces):
        factor, fresh_term = pieces
        return (factor[None, :, None] * carried + fresh_term, carried)

    final_carry, starts = lax.scan(
        carry_step,
        start_state.reshape(states, head_count, head_width),
        (block_totals, block_states),
    )
    outer_part = (
        jnp.einsum("cihn,cnhp->cihp", c_head, starts, precision=highest)
        * jnp.exp(decays)[..., None]
    )
    result = inner_part + outer_part + skip_gain[None, None, :, None] * values
    return (
        result.reshape(length, head_count * head_width),
        final_carry.reshape(states, head_count * head_width),
    )


def gate_values(result, gate_rows):
    gate_rows = gate_rows.astype(jnp.float32)
    return result * gate_rows * jax.nn.sigmoid(gate_rows)


def select_heads(c_rows, owners):
    shape_front = c_rows.shape[:2]
    states = c_rows.shape[2] // G
    grouped = c_rows.reshape(shape_front[0], shape_front[1], G, states)
    return jnp.take(grouped, owners, axis=2)


def body(
    x_pre,
    z_pre,
    b_pre,
    c_pre,
    dt_pre,
    lengths,
    init_state,
    a_rates,
    dt_bias,
    skip_scale,
    norm_gain,
    x_dec,
    z_dec,
    b_dec,
    c_dec,
    dt_dec,
):
    heads_here = a_rates.shape[0]
    head_width = x_pre.shape[2] // heads_here
    first_head = lax.axis_index("head") * heads_here
    owners = group_owners(first_head, heads_here)
    picker = group_pick(owners)
    length = x_pre.shape[1]
    positions = jnp.arange(length, dtype=jnp.int32)
    valid_mask = (positions[None, :] < lengths[:, None]).astype(jnp.float32)
    step_delta = jax.nn.softplus(dt_pre + dt_bias) * valid_mask[:, :, None]

    def one_prompt(pieces):
        inputs, b_rows, c_rows, prompt_delta, start_state = pieces
        return scan_prompt(
            inputs, b_rows, c_rows, prompt_delta, a_rates, skip_scale, start_state, owners
        )

    result, final_carry = lax.map(one_prompt, (x_pre, b_pre, c_pre, step_delta, init_state))
    final_state = final_carry.astype(jnp.bfloat16)
    gated_rows = gate_values(result, z_pre)
    pre_totals = lax.psum(jnp.sum(gated_rows * gated_rows, axis=-1), "head")
    norm_scale = lax.rsqrt(pre_totals[:, :, None] / (H * P_SIZE) + epsilon)
    out_pre = (gated_rows * norm_scale * norm_gain * valid_mask[:, :, None]).astype(jnp.bfloat16)
    slots_here = x_dec.shape[0]
    prompt_count = x_dec.shape[1]
    prompts_here = final_state.shape[0]
    states = final_state.shape[1]
    cached = final_state.reshape(prompts_here, states, heads_here, head_width)
    queries = lax.all_to_all(c_dec, "sample", split_axis=1, concat_axis=0, tiled=True)
    c_head = select_heads(queries, owners)
    answers = jnp.einsum("sphn,pnhq->sphq", c_head, cached, preferred_element_type=jnp.float32)
    answers = answers.reshape(answers.shape[0], prompts_here, heads_here * head_width)
    state_reads = lax.all_to_all(
        answers.astype(jnp.bfloat16), "sample", split_axis=0, concat_axis=1, tiled=True
    ).astype(answers.dtype)
    state_reads = state_reads.reshape(slots_here, prompt_count, heads_here, head_width)
    c_groups = c_dec.astype(jnp.float32).reshape(slots_here, prompt_count, G, states)
    b_groups = b_dec.astype(jnp.float32).reshape(slots_here, prompt_count, G, states)
    cb_dot = jnp.einsum("spgn,spgn->spg", c_groups, b_groups, precision=highest)
    cb_dot = jnp.einsum("spg,hg->sph", cb_dot, picker, precision=highest)
    step_sizes = jax.nn.softplus(dt_dec + dt_bias)
    decay_rate = jnp.exp(-step_sizes * a_rates)
    values = x_dec.astype(jnp.float32).reshape(slots_here, prompt_count, heads_here, head_width)
    fresh_term = (
        decay_rate[..., None] * state_reads + (step_sizes * cb_dot + skip_scale)[..., None] * values
    )
    gated_dec = gate_values(
        fresh_term.reshape(slots_here, prompt_count, heads_here * head_width), z_dec
    )
    dec_totals = lax.psum(jnp.sum(gated_dec * gated_dec, axis=-1), "head")
    dec_scale = lax.rsqrt(dec_totals[:, :, None] / (H * P_SIZE) + epsilon)
    out_dec = (gated_dec * dec_scale * norm_gain).astype(jnp.bfloat16)
    return (out_pre, final_state, out_dec)


def solution(mesh):
    in_specs = (
        P(("rep", "sample"), None, "head"),
        P(("rep", "sample"), None, "head"),
        P(("rep", "sample"), None, None),
        P(("rep", "sample"), None, None),
        P(("rep", "sample"), None, "head"),
        P(("rep", "sample")),
        P(("rep", "sample"), None, "head"),
        P("head"),
        P("head"),
        P("head"),
        P("head"),
        P(("rep", "sample"), None, "head"),
        P(("rep", "sample"), None, "head"),
        P(("rep", "sample"), None, None),
        P(("rep", "sample"), None, None),
        P(("rep", "sample"), None, "head"),
    )
    out_specs = (
        P(("rep", "sample"), None, "head"),
        P(("rep", "sample"), None, "head"),
        P(("rep", "sample"), None, "head"),
    )
    return jax.shard_map(body, mesh=mesh, in_specs=in_specs, out_specs=out_specs, check_vma=False)
```

profile of v0, /device:TPU:0, one launch (start us, length us, event | category | flops | bytes accessed | tf_op | source)
XLA Modules:
  0.0 61.4 jit_solution(16359119723385610459)
XLA Ops:
  0.7 0.8 %copy.168 = bf16[1,4,512]{2,0,1:T(2,128)(2,1)S(1)} copy(bf16[1,4,512]{2,1,0:T(4,128)(2,1)} %param.32) | data formatting | bytes 8192 | tf_op args[14]
  1.4 0.5 broadcast.360
  1.9 0.7 %reduce.6 = bf16[4,512]{1,0:T(4,128)(2,1)S(1)} reduce(bf16[4,1,512]{2,1,0:T(2,128)(2,1)S(1)} %bitcast.142, bf16[]{:T(256)} %broadcast.360), dimensions={1}, to_apply=%bitcast.126.reduce_sub_computation | reduce | bytes 8194
  2.6 0.6 reshape.510
  3.2 6.3 %all-to-all-start = ((bf16[4,2,256]{2,1,0:T(2,128)(2,1)}), bf16[4,2,256]{2,1,0:T(2,128)(2,1)}, u32[]{:S(2)}, u32[]{:S(2)}) async-start(bf16[4,2,256]{2,1,0:T(2,128)(2,1)} %reshape.510), calls=%async_computation | async-start | bytes 8192 | tf_op jit(solution)/shard_map/all_to_all | solution.py:128
  10.2 0.8 %negate_multiply_fusion = f32[1,128,32]{1,2,0:T(8,128)S(1)} fusion(f32[32]{0:T(128)} %param.25, f32[128]{0:T(128)S(1)} %compare_convert_fusion, f32[1,128,32]{1,2,0:T(8,128)} %param.22, f32[32]{0:T(128)} %param.26), kind=kLoop, calls=%fused_computation.73 | loop fusion | flops 40960 | bytes 33536 | tf_op jit(solution)/shard_map/while/body/eval_jaxpr/mul | solution.py:39
  11.0 0.1 copy.124
  11.1 0.2 reduce_window_sum.12
  11.3 0.1 copy.138
  11.4 0.6 compare_and_fusion
  11.9 0.6 iota_compare_fusion
  12.6 0.6 compare_select_fusion.3
  13.2 0.9 %reshape.439 = bf16[128,4,128]{2,1,0:T(4,128)(2,1)S(1)} reshape(bf16[1,128,512]{2,1,0:T(8,128)(2,1)} %param.21) | data formatting | bytes 262144 | tf_op jit(solution)/shard_map/reshape.21
  14.1 1.0 %copy.129 = bf16[1,128,512]{1,2,0:T(8,128)(2,1)S(1)} copy(bf16[1,128,512]{2,1,0:T(8,128)(2,1)} %param.21) | data formatting | bytes 262144 | tf_op args[3]
  15.2 2.0 %copy.127 = bf16[1,128,2048]{1,2,0:T(8,128)(2,1)} copy(bf16[1,128,2048]{2,1,0:T(8,128)(2,1)} %param.18) | data formatting | bytes 1048576 | tf_op args[0]
  17.2 1.2 %copy.133 = f32[1,128,2048]{1,2,0:T(8,128)} copy(bf16[1,128,2048]{2,1,0:T(8,128)(2,1)S(1)} %copy-done.2) | data formatting | bytes 1572864 | tf_op jit(solution)/shard_map/while/body/eval_jaxpr/convert_element_type | solution.py:37
  18.4 0.8 %copy.136 = bf16[1,128,512]{1,2,0:T(8,128)(2,1)} copy(bf16[1,128,512]{2,1,0:T(8,128)(2,1)S(1)} %copy-done.6) | data formatting | bytes 262144 | tf_op args[2]
  19.2 0.5 fusion.59
  19.7 0.6 reshape.449
  20.3 0.7 %copy.125 = f32[128,32]{0,1:T(8,128)} copy(f32[128,32]{1,0:T(8,128)S(1)} %bitcast.135) | data formatting | bytes 32768 | tf_op jit(solution)/shard_map/while/body/eval_jaxpr/sub | solution.py:41
  21.0 0.6 pad_clamp_fusion.1
  21.6 0.1 copy.132
  21.7 0.6 pad_clamp_fusion
  22.3 0.1 copy.130
  22.4 0.3 copy.131
  22.8 0.7 %multiply_bitcast_fusion = (f32[128,32]{0,1:T(8,128)}, f32[128,32]{0,1:T(8,128)}) fusion(f32[1,128,32]{1,2,0:T(8,128)S(1)} %copy.138, f32[32]{0:T(128)S(1)} %slice_bitcast_fusion, f32[128]{0:T(128)S(1)} %compare_convert_fusion, f32[1,128,32]{1,2,0:T(8,128)S(1)} %copy-done.8, f32[32]{0:T(128)S(1)} %copy-done.18), kind=kLoop, calls=%fused_computation.72 | loop fusion | flops 40960 | bytes 66304 | tf_op jit(solution)/shard_map/while/body/eval_jaxpr/mul | solution.py:47
  23.5 0.2 convolution_bitcast_fusion.1
  23.7 0.8 %gather_fusion = f32[32,128,128]{1,2,0:T(8,128)S(1)} fusion(f32[128,128,4]{0,1,2:T(8,128)S(1)} %convolution_bitcast_fusion.1, s32[1024]{0:T(1024)} %pad_clamp_fusion.1), kind=kCustom, calls=%fused_computation.2 | custom fusion | bytes 4194432 | tf_op jit(solution)/shard_map/while/body/eval_jaxpr/jit(_take)/gather | solution.py:34
  24.5 1.9 %gather_fusion.2 = bf16[32,128,128]{2,1,0:T(8,128)(2,1)} fusion(bf16[128,4,128]{2,0,1:T(8,128)(2,1)S(1)} %bitcast.129, s32[1024]{0:T(1024)} %pad_clamp_fusion), kind=kCustom, calls=%fused_computation.clone | custom fusion | bytes 2097280 | tf_op jit(solution)/shard_map/while/body/eval_jaxpr/jit(_take)/gather | solution.py:36
  26.5 4.0 %fusion.12 = f32[1,128,32,64]{1,3,2,0:T(8,128)S(1)} fusion(bf16[128,32,64]{0,2,1:T(8,128)(2,1)} %bitcast.137, f32[32,128,128]{1,2,0:T(8,128)S(1)} %gather_fusion, f32[128,32]{0,1:T(8,128)S(1)} %copy-done.17, f32[128,32]{0,1:T(8,128)S(1)} %copy-done.12, pred[32]{0:T(512)(128)(4,1)S(1)} %copy-done.26, pred[128,128]{0,1:T(8,128)(4,1)S(1)} %copy-done.14), kind=kOutput, calls=%fused_computation.16 | convolution fusion | flops 405798912 | bytes 3719200 | tf_op jit(solution)/shard_map/while/body/eval_jaxpr/cijh,cjhp->cihp/dot_general | solution.py:44
  30.5 2.2 %fusion.17 = f32[1,128,32,64]{1,3,2,0:T(8,128)S(1)} fusion(f32[1,128,32,64]{1,3,2,0:T(8,128)S(1)} %fusion.12, f32[128,32,64]{0,2,1:T(8,128)S(1)} %bitcast.131, bf16[32,128,128]{2,1,0:T(8,128)(2,1)S(1)} %copy-done, f32[1,128,32,64]{1,3,2,0:T(8,128)S(1)} %bitcast.132, pred[32]{0:T(512)(128)(4,1)S(1)} %copy-done.26, f32[32]{0:T(128)S(1)} %copy-done.25, ...), kind=kOutput, calls=%fused_computation.20 | convolution fusion | flops 404226048 | bytes 5259424 | tf_op jit(solution)/shard_map/while/body/eval_jaxpr/cihn,cnhp->cihp/dot_general | solution.py:61
  32.7 0.0 copy-start.7
  32.8 0.0 copy-start.19
  32.8 0.0 copy-start.23
  32.8 0.3 copy.134
  33.1 0.0 copy-start.3
  33.2 0.5 copy-done.7
  33.6 0.1 copy.137
  33.8 1.8 %gather_fusion.3 = bf16[32,128,128]{2,1,0:T(8,128)(2,1)} fusion(bf16[128,4,128]{2,0,1:T(8,128)(2,1)S(1)} %bitcast.130, s32[1024]{0:T(1024)} %pad_clamp_fusion), kind=kCustom, calls=%fused_computation.1.clone | custom fusion | bytes 2097280 | tf_op jit(solution)/shard_map/while/body/eval_jaxpr/jit(_take)/gather | solution.py:35
  35.6 0.1 mul.246
  35.6 0.1 mul.247
  35.8 0.4 multiply_reduce_fusion
  36.2 2.7 %fusion = f32[32,128,64]{1,2,0:T(8,128)S(1)} fusion(bf16[128,32,64]{0,2,1:T(8,128)(2,1)S(1)} %bitcast.138, bf16[32,128,128]{2,1,0:T(8,128)(2,1)} %gather_fusion.3, f32[128,32]{0,1:T(8,128)S(1)} %copy-done.16, pred[32]{0:T(512)(128)(4,1)S(1)} %copy-done.27), kind=kOutput, calls=%fused_computation.4 | convolution fusion | flops 404226048 | bytes 2637856 | tf_op jit(solution)/shard_map/while/body/eval_jaxpr/cjhn,cjhp->cnhp/dot_general | solution.py:46
  39.0 0.4 fusion.26
  39.4 0.1 fusion.51
  39.5 0.7 %reshape.511 = bf16[4,1,512]{2,1,0:T(2,128)(2,1)S(1)} reshape(bf16[4,2,256]{2,1,0:T(2,128)(2,1)} %all-to-all-done) | data formatting | bytes 8192
  40.2 0.7 %gather_fusion.1 = bf16[32,4,128]{2,1,0:T(4,128)(2,1)S(1)} fusion(bf16[4,4,128]{2,0,1:T(4,128)(2,1)S(1)} %bitcast.141, s32[1024]{0:T(1024)} %pad_clamp_fusion.1), kind=kCustom, calls=%fused_computation.3 | custom fusion | bytes 65664 | tf_op jit(solution)/shard_map/jit(_take)/gather | solution.py:80
  41.0 0.4 fusion.18
  41.4 0.1 convert_element_type.108
  41.5 0.7 %reduce.7 = bf16[4,2048]{1,0:T(4,128)(2,1)S(1)} reduce(bf16[4,1,2048]{2,1,0:T(2,128)(2,1)S(1)} %convert_element_type.108, bf16[]{:T(256)} %broadcast.360), dimensions={1}, to_apply=%convert_element_type.108.reduce_sub_computation | reduce | bytes 32770 | tf_op jit(solution)/shard_map/convert_element_type | solution.py:133
  42.2 0.6 %reshape.512 = bf16[4,2,1024]{2,1,0:T(2,128)(2,1)} reshape(bf16[4,2048]{1,0:T(4,128)(2,1)S(1)} %reduce.7) | data formatting | bytes 32768
  42.8 5.1 %all-to-all-start.1 = ((bf16[4,2,1024]{2,1,0:T(2,128)(2,1)}), bf16[4,2,1024]{2,1,0:T(2,128)(2,1)S(1)}, u32[]{:S(2)}, u32[]{:S(2)}) async-start(bf16[4,2,1024]{2,1,0:T(2,128)(2,1)} %reshape.512), calls=%async_computation.1 | async-start | bytes 32768 | tf_op jit(solution)/shard_map/all_to_all | solution.py:132
  47.9 0.2 fusion.21
  48.1 1.0 %copy.145 = bf16[1,128,2048]{2,1,0:T(8,128)(2,1)} copy(bf16[1,128,2048]{1,2,0:T(8,128)(2,1)S(1)} %fusion.26) | data formatting | bytes 1048576
  49.2 0.1 mul.262
  49.2 0.1 mul.263
  49.3 0.1 mul.257
  49.4 0.1 mul.258
  49.5 4.0 %all-to-all-done.1 = bf16[4,2,1024]{2,1,0:T(2,128)(2,1)S(1)} async-done(((bf16[4,2,1024]{2,1,0:T(2,128)(2,1)}), bf16[4,2,1024]{2,1,0:T(2,128)(2,1)S(1)}, u32[]{:S(2)}, u32[]{:S(2)}) %all-to-all-start.1) | async-done | bytes 16416 | tf_op jit(solution)/shard_map/all_to_all | solution.py:132
  53.6 0.2 multiply_reduce_fusion.1
  53.8 5.6 %all-reduce = (f32[1,128]{1,0:T(1,128)S(1)}, f32[1,4]{1,0:T(1,128)S(1)}) all-reduce(f32[1,128]{1,0:T(1,128)S(1)} %bitcast.143, f32[1,4]{1,0:T(1,128)S(1)} %bitcast.144), channel_id=1, replica_groups=mesh['rep'=2,'sample'=4,'head'=4] {'head'}, use_global_device_ids=true, to_apply=%region_2.4 | all-reduce | flops 132 | bytes 1056 | tf_op jit(solution)/shard_map/psum | solution.py:120
  59.5 0.1 multiply_convert_fusion.1
  59.6 0.6 %copy.146 = bf16[1,4,2048]{2,1,0:T(4,128)(2,1)} copy(bf16[1,4,2048]{2,0,1:T(2,128)(2,1)S(1)} %multiply_convert_fusion.1) | data formatting | bytes 32768
  60.2 1.2 %multiply_convert_fusion = bf16[1,128,2048]{2,1,0:T(8,128)(2,1)} fusion(f32[128]{0:T(128)S(1)} %copy-done.21, f32[2048]{0:T(1024)S(1)} %copy-done.9, f32[128]{0:T(128)S(1)} %rsqrt_bitcast_fusion.1, f32[1,128,2048]{2,1,0:T(8,128)S(1)} %copy.134, bf16[1,128,2048]{2,1,0:T(8,128)(2,1)S(1)} %copy-done.3), kind=kLoop, calls=%fused_computation.41 | loop fusion | flops 2621440 | bytes 2106368 | tf_op jit(solution)/shard_map/convert_element_type | solution.py:122
  (68 shorter events, 0.3 us)
Async XLA Ops:
  0.6 16.6 %copy-start.2 = (bf16[1,128,2048]{2,1,0:T(8,128)(2,1)S(1)}, bf16[1,128,2048]{2,1,0:T(8,128)(2,1)}, u32[]{:S(2)}) copy-start(bf16[1,128,2048]{2,1,0:T(8,128)(2,1)} %param.18) | copy-start | bytes 1572868
  0.6 17.8 %copy-start.6 = (bf16[1,128,512]{2,1,0:T(8,128)(2,1)S(1)}, bf16[1,128,512]{2,1,0:T(8,128)(2,1)}, u32[]{:S(2)}) copy-start(bf16[1,128,512]{2,1,0:T(8,128)(2,1)} %param.20) | copy-start | bytes 393220
  1.9 17.8 %copy-start.13 = (bf16[1,4,512]{2,1,0:T(4,128)(2,1)S(1)}, bf16[1,4,512]{2,1,0:T(4,128)(2,1)}, u32[]{:S(2)}) copy-start(bf16[1,4,512]{2,1,0:T(4,128)(2,1)} %param.32) | copy-start | bytes 12292
  3.2 36.3 %all-to-all-start = ((bf16[4,2,256]{2,1,0:T(2,128)(2,1)}), bf16[4,2,256]{2,1,0:T(2,128)(2,1)}, u32[]{:S(2)}, u32[]{:S(2)}) async-start(bf16[4,2,256]{2,1,0:T(2,128)(2,1)} %reshape.510), calls=%async_computation | async-start | bytes 8192 | tf_op jit(solution)/shard_map/all_to_all | solution.py:128
  10.2 12.5 %copy-start.20 = (f32[128]{0:T(128)}, f32[128]{0:T(128)S(1)}, u32[]{:S(2)}) copy-start(f32[128]{0:T(128)S(1)} %compare_convert_fusion) | copy-start | bytes 1540
  12.6 9.8 %copy-start.4 = (f32[1,128,2048]{2,1,0:T(8,128)S(1)}, f32[1,128,2048]{2,1,0:T(8,128)}, u32[]{:S(2)}) copy-start(f32[1,128,2048]{2,1,0:T(8,128)} %param.24) | copy-start | bytes 3145732
  17.2 5.6 %copy-start.8 = (f32[1,128,32]{1,2,0:T(8,128)S(1)}, f32[1,128,32]{1,2,0:T(8,128)}, u32[]{:S(2)}) copy-start(f32[1,128,32]{1,2,0:T(8,128)} %param.22) | copy-start | bytes 49156
  17.2 5.6 %copy-start.18 = (f32[32]{0:T(128)S(1)}, f32[32]{0:T(128)}, u32[]{:S(2)}) copy-start(f32[32]{0:T(128)} %param.26) | copy-start | bytes 388
  24.5 2.0 %copy-start.12 = (f32[128,32]{0,1:T(8,128)S(1)}, f32[128,32]{0,1:T(8,128)}, u32[]{:S(2)}) copy-start(f32[128,32]{0,1:T(8,128)} %copy.125) | copy-start | bytes 49156
  24.5 2.0 %copy-start.14 = (pred[128,128]{0,1:T(8,128)(4,1)S(1)}, pred[128,128]{0,1:T(8,128)(4,1)}, u32[]{:S(2)}) copy-start(pred[128,128]{0,1:T(8,128)(4,1)} %iota_compare_fusion) | copy-start | bytes 49156
  24.5 2.0 %copy-start.17 = (f32[128,32]{0,1:T(8,128)S(1)}, f32[128,32]{0,1:T(8,128)}, u32[]{:S(2)}) copy-start(f32[128,32]{0,1:T(8,128)} %get-tuple-element.77) | copy-start | bytes 49156
  24.5 2.0 %copy-start.26 = (pred[32]{0:T(512)(128)(4,1)S(1)}, pred[32]{0:T(512)(128)(4,1)}, u32[]{:S(2)}) copy-start(pred[32]{0:T(512)(128)(4,1)} %compare_and_fusion) | copy-start | bytes 100
  26.5 4.0 %copy-start = (bf16[32,128,128]{2,1,0:T(8,128)(2,1)S(1)}, bf16[32,128,128]{2,1,0:T(8,128)(2,1)}, u32[]{:S(2)}) copy-start(bf16[32,128,128]{2,1,0:T(8,128)(2,1)} %gather_fusion.2) | copy-start | bytes 3145732
  26.5 4.0 %copy-start.1 = (f32[1,128,2048]{1,2,0:T(8,128)S(1)}, f32[1,128,2048]{1,2,0:T(8,128)}, u32[]{:S(2)}) copy-start(f32[1,128,2048]{1,2,0:T(8,128)} %copy.133) | copy-start | bytes 3145732
  26.5 4.0 %copy-start.25 = (f32[32]{0:T(128)S(1)}, f32[32]{0:T(128)}, u32[]{:S(2)}) copy-start(f32[32]{0:T(128)} %param.27) | copy-start | bytes 388
  32.7 0.9 %copy-start.7 = (bf16[1,128,512]{1,2,0:T(8,128)(2,1)S(1)}, bf16[1,128,512]{1,2,0:T(8,128)(2,1)}, u32[]{:S(2)}) copy-start(bf16[1,128,512]{1,2,0:T(8,128)(2,1)} %copy.136) | copy-start | bytes 393220
  32.7 2.8 %copy-start.28 = (f32[32]{0:T(128)S(1)}, f32[32]{0:T(128)}, u32[]{:S(2)}) copy-start(f32[32]{0:T(128)} %fusion.59) | copy-start | bytes 388
  32.8 3.0 %copy-start.22 = (bf16[1,4,512]{2,1,0:T(4,128)(2,1)S(1)}, bf16[1,4,512]{2,1,0:T(4,128)(2,1)}, u32[]{:S(2)}) copy-start(bf16[1,4,512]{2,1,0:T(4,128)(2,1)} %param.31) | copy-start | bytes 12292
  32.8 3.0 %copy-start.19 = (f32[32]{0:T(128)S(1)}, f32[32]{0:T(128)}, u32[]{:S(2)}) copy-start(f32[32]{0:T(128)} %param.26) | copy-start | bytes 388
  32.8 3.0 %copy-start.23 = (f32[32]{0:T(128)S(1)}, f32[32]{0:T(128)}, u32[]{:S(2)}) copy-start(f32[32]{0:T(128)} %param.25) | copy-start | bytes 388
  32.8 2.9 %copy-start.24 = (f32[1,4,32]{2,1,0:T(4,128)S(1)}, f32[1,4,32]{2,1,0:T(4,128)}, u32[]{:S(2)}) copy-start(f32[1,4,32]{2,1,0:T(4,128)} %param.33) | copy-start | bytes 1540
  33.1 2.6 %copy-start.3 = (bf16[1,128,2048]{2,1,0:T(8,128)(2,1)S(1)}, bf16[1,128,2048]{2,1,0:T(8,128)(2,1)}, u32[]{:S(2)}) copy-start(bf16[1,128,2048]{2,1,0:T(8,128)(2,1)} %param.19) | copy-start | bytes 1572868
  33.2 3.0 %copy-start.5 = (bf16[1,128,2048]{1,2,0:T(8,128)(2,1)S(1)}, bf16[1,128,2048]{1,2,0:T(8,128)(2,1)}, u32[]{:S(2)}) copy-start(bf16[1,128,2048]{1,2,0:T(8,128)(2,1)} %copy.127) | copy-start | bytes 1572868
  33.2 3.0 %copy-start.16 = (f32[128,32]{0,1:T(8,128)S(1)}, f32[128,32]{0,1:T(8,128)}, u32[]{:S(2)}) copy-start(f32[128,32]{0,1:T(8,128)} %get-tuple-element.76) | copy-start | bytes 49156
  33.2 3.0 %copy-start.27 = (pred[32]{0:T(512)(128)(4,1)S(1)}, pred[32]{0:T(512)(128)(4,1)}, u32[]{:S(2)}) copy-start(pred[32]{0:T(512)(128)(4,1)} %compare_and_fusion) | copy-start | bytes 100
  36.2 3.2 %copy-start.15 = (bf16[4,4,128]{2,1,0:T(4,128)(2,1)S(1)}, bf16[4,4,128]{2,1,0:T(4,128)(2,1)}, u32[]{:S(2)}) copy-start(bf16[4,4,128]{2,1,0:T(4,128)(2,1)} %reshape.449) | copy-start | bytes 12292
  39.0 9.0 %copy-start.29 = (s32[32]{0:T(128)S(1)}, s32[32]{0:T(128)}, u32[]{:S(2)}) copy-start(s32[32]{0:T(128)} %get-tuple-element.79) | copy-start | bytes 388
  39.0 14.6 %copy-start.10 = (bf16[1,4,2048]{2,1,0:T(4,128)(2,1)S(1)}, bf16[1,4,2048]{2,1,0:T(4,128)(2,1)}, u32[]{:S(2)}) copy-start(bf16[1,4,2048]{2,1,0:T(4,128)(2,1)} %param.30) | copy-start | bytes 49156
  39.0 14.6 %copy-start.11 = (bf16[1,4,2048]{2,1,0:T(4,128)(2,1)S(1)}, bf16[1,4,2048]{2,1,0:T(4,128)(2,1)}, u32[]{:S(2)}) copy-start(bf16[1,4,2048]{2,1,0:T(4,128)(2,1)} %param.29) | copy-start | bytes 49156
  39.0 20.5 %copy-start.9 = (f32[2048]{0:T(1024)S(1)}, f32[2048]{0:T(1024)}, u32[]{:S(2)}) copy-start(f32[2048]{0:T(1024)} %param.28) | copy-start | bytes 24580
  39.0 21.2 %copy-start.21 = (f32[128]{0:T(128)S(1)}, f32[128]{0:T(128)}, u32[]{:S(2)}) copy-start(f32[128]{0:T(128)} %copy-done.20) | copy-start | bytes 1540
  42.8 10.7 %all-to-all-start.1 = ((bf16[4,2,1024]{2,1,0:T(2,128)(2,1)}), bf16[4,2,1024]{2,1,0:T(2,128)(2,1)S(1)}, u32[]{:S(2)}, u32[]{:S(2)}) async-start(bf16[4,2,1024]{2,1,0:T(2,128)(2,1)} %reshape.512), calls=%async_computation.1 | async-start | bytes 32768 | tf_op jit(solution)/shard_map/all_to_all | solution.py:132
where the time goes:
time: 62.1 us; the launch traced here: 61.4 us
  local copies, waits for them, and re-layouts  20.3 us (33%)
  starting transfers between devices  11.4 us (18%)
  matrix products  9.71 us (16%)
  other arithmetic  8.5 us (14%)
  blocking collectives  5.63 us (9%)
  waiting for transfers between devices  4.02 us (6%)
  between operations  1.81 us (3%)
    unnamed x72, local copies, waits for them, and re-layouts  9.6 us
    all_to_all x1, starting transfers between devices, body(): lax.all_to_all(c_dec, 'sample', split_axis=1, concat_axis=0, tiled=True)  6.35 us
    psum x1, blocking collectives, body(): pre_totals = lax.psum(jnp.sum(gated_rows * gated_rows, axis=-1), 'head')  5.63 us
    all_to_all x1, starting transfers between devices, body(): lax.all_to_all(answers.astype(jnp.bfloat16), 'sample', split_axis=0, conc...  5.09 us
    all_to_all x1, waiting for transfers between devices, body(): lax.all_to_all(answers.astype(jnp.bfloat16), 'sample', split_axis=0, conc...  4.01 us
    dot_general x1, matrix products, scan_prompt(): jnp.einsum('cijh,cjhp->cihp', scores, values, precision=highest)  3.96 us
    dot_general x1, matrix products, scan_prompt(): jnp.einsum('cjhn,cjhp->cnhp', b_head * tail_decay[..., None], values, pre...  2.73 us
    dot_general x1, matrix products, scan_prompt(): jnp.einsum('cihn,cnhp->cihp', c_head, starts, precision=highest)  2.2 us
  transfers between devices with their start and end apart: 2, of which 1 were waited for; matrix products, arithmetic and copies ran while one was open for 49% of the time, Pallas kernels for 0%

commit v1 on v0

--- a/solution.py
+++ b/solution.py
@@ -125,7 +125,12 @@
     prompts_here = final_state.shape[0]
     states = final_state.shape[1]
     cached = final_state.reshape(prompts_here, states, heads_here, head_width)
-    queries = lax.all_to_all(c_dec, "sample", split_axis=1, concat_axis=0, tiled=True)
+    queries = jnp.concatenate(
+        lax.all_to_all(
+            jnp.stack(jnp.split(c_dec, lax.axis_size("sample"), axis=1)), "sample", 0, 0
+        ),
+        axis=0,
+    )
     c_head = select_heads(queries, owners)
     answers = jnp.einsum("sphn,pnhq->sphq", c_head, cached, preferred_element_type=jnp.float32)
     answers = answers.reshape(answers.shape[0], prompts_here, heads_here * head_width)

time: 62.1 us -> 64.5 us (1.039)
  local copies, waits for them, and re-layouts: 20.3 us -> 21.9 us
  other arithmetic: 8.5 us -> 9.29 us
    another operation x4 -> x6, local copies, waits for them, and re-layouts: 1.59 us -> 3.06 us
    unnamed x72 -> x64, local copies, waits for them, and re-layouts: 9.6 us -> 8.68 us
    mul x1, other arithmetic: 0.71 us -> 1.44 us  [scan_prompt(): b_head * tail_decay[..., None]]
    another operation x0 -> x2, other arithmetic: none -> 0.73 us  [body(): jnp.stack(jnp.split(c_dec, lax.axis_size('sample'), axis=1))]
    unnamed x1 -> x0, other arithmetic: 0.67 us -> none
  transfers between devices with their start and end apart: 2 -> 2, of which waited for: 1 -> 1; matrix products, arithmetic and copies ran while one was open for 49% -> 50% of each run, Pallas kernels for 0% -> 0%
where the time goes in v1:
time: 64.5 us; the launch traced here: 63.8 us
  local copies, waits for them, and re-layouts  21.9 us (34%)
  starting transfers between devices  11.4 us (18%)
  matrix products  9.73 us (15%)
  other arithmetic  9.29 us (14%)
  blocking collectives  5.63 us (9%)
  waiting for transfers between devices  4.02 us (6%)
  between operations  1.78 us (3%)
    unnamed x64, local copies, waits for them, and re-layouts  8.68 us
    all_to_all x1, starting transfers between devices, body(): lax.all_to_all(jnp.stack(jnp.split(c_dec, lax.axis_size('sample'), axis=1...  6.35 us
    psum x1, blocking collectives, body(): pre_totals = lax.psum(jnp.sum(gated_rows * gated_rows, axis=-1), 'head')  5.63 us
    all_to_all x1, starting transfers between devices, body(): lax.all_to_all(answers.astype(jnp.bfloat16), 'sample', split_axis=0, conc...  5.09 us
    all_to_all x1, waiting for transfers between devices, body(): lax.all_to_all(answers.astype(jnp.bfloat16), 'sample', split_axis=0, conc...  4.01 us
    dot_general x1, matrix products, scan_prompt(): jnp.einsum('cijh,cjhp->cihp', scores, values, precision=highest)  3.96 us
    dot_general x1, matrix products, scan_prompt(): jnp.einsum('cjhn,cjhp->cnhp', b_head * tail_decay[..., None], values, pre...  2.73 us
    dot_general x1, matrix products, scan_prompt(): jnp.einsum('cihn,cnhp->cihp', c_head, starts, precision=highest)  2.2 us
  transfers between devices with their start and end apart: 2, of which 1 were waited for; matrix products, arithmetic and copies ran while one was open for 50% of the time, Pallas kernels for 0%

profile of v1, /device:TPU:0, one launch (start us, length us, event | category | flops | bytes accessed | tf_op | source)
XLA Modules:
  0.0 63.8 jit_solution(543395055968481401)
XLA Ops:
  0.6 0.0 copy-start.2
  0.7 0.9 %slice_bitcast_fusion.3 = (bf16[1,1,1,512]{3,2,1,0:T(2,128)(2,1)S(1)}, bf16[1,1,1,512]{3,2,1,0:T(2,128)(2,1)S(1)}, bf16[1,1,1,512]{3,2,1,0:T(2,128)(2,1)S(1)}, bf16[1,1,1,512]{3,2,1,0:T(2,128)(2,1)S(1)}) fusion(bf16[1,4,512]{2,1,0:T(4,128)(2,1)} %param.32), kind=kLoop, calls=%fused_computation.86 | loop fusion | bytes 8192 | tf_op jit(solution)/shard_map/stack | solution.py:130
  1.6 0.6 broadcast.360
  2.2 0.7 %reduce.5 = bf16[4,512]{1,0:T(4,128)(2,1)S(1)} reduce(bf16[4,1,1,512]{3,2,1,0:T(2,128)(2,1)S(1)} %pad_maximum_fusion, bf16[]{:T(256)} %broadcast.360), dimensions={1,2}, to_apply=%pad_maximum_fusion.reduce_sub_computation | reduce | bytes 8194 | tf_op jit(solution)/shard_map/stack | solution.py:130
  2.9 0.6 reshape.502
  3.5 6.3 %all-to-all-start = ((bf16[4,2,256]{2,1,0:T(2,128)(2,1)}), bf16[4,2,256]{2,1,0:T(2,128)(2,1)}, u32[]{:S(2)}, u32[]{:S(2)}) async-start(bf16[4,2,256]{2,1,0:T(2,128)(2,1)} %reshape.502), calls=%async_computation | async-start | bytes 8192 | tf_op jit(solution)/shard_map/all_to_all | solution.py:129
  10.5 0.5 copy-done.17
  11.0 0.8 %negate_multiply_fusion = f32[1,128,32]{1,2,0:T(8,128)S(1)} fusion(f32[32]{0:T(128)} %param.25, f32[128]{0:T(128)S(1)} %compare_convert_fusion, f32[1,128,32]{1,2,0:T(8,128)} %param.22, f32[32]{0:T(128)} %param.26), kind=kLoop, calls=%fused_computation.73 | loop fusion | flops 40960 | bytes 33536 | tf_op jit(solution)/shard_map/while/body/eval_jaxpr/mul | solution.py:39
  11.8 0.1 copy.100
  11.9 0.2 reduce_window_sum.12
  12.1 0.7 %copy.114 = f32[1,128,32]{1,2,0:T(8,128)} copy(f32[1,128,32]{2,1,0:T(8,128)S(1)} %reduce_window_sum.12) | data formatting | bytes 32768 | tf_op jit(solution)/shard_map/while/body/eval_jaxpr/jit(cumsum)/reduce_window_sum | solution.py:39
  12.8 0.6 slice_bitcast_fusion.4
  13.4 0.5 compare_and_fusion
  13.9 0.6 iota_compare_fusion
  14.5 0.9 %reshape.432 = bf16[128,4,128]{2,1,0:T(4,128)(2,1)S(1)} reshape(bf16[1,128,512]{2,1,0:T(8,128)(2,1)} %param.21) | data formatting | bytes 262144 | tf_op jit(solution)/shard_map/reshape.21
  15.5 1.0 %copy.105 = bf16[1,128,512]{1,2,0:T(8,128)(2,1)S(1)} copy(bf16[1,128,512]{2,1,0:T(8,128)(2,1)} %param.21) | data formatting | bytes 262144 | tf_op args[3]
  16.5 0.6 compare_select_fusion.3
  17.1 2.0 %copy.103 = bf16[1,128,2048]{1,2,0:T(8,128)(2,1)} copy(bf16[1,128,2048]{2,1,0:T(8,128)(2,1)} %param.18) | data formatting | bytes 1048576 | tf_op args[0]
  19.1 1.2 %copy.109 = f32[1,128,2048]{1,2,0:T(8,128)} copy(bf16[1,128,2048]{2,1,0:T(8,128)(2,1)S(1)} %copy-done.2) | data formatting | bytes 1572864 | tf_op jit(solution)/shard_map/while/body/eval_jaxpr/convert_element_type | solution.py:37
  20.3 0.6 reshape.441
  20.9 0.6 fusion.59
  21.5 0.8 %copy.112 = bf16[1,128,512]{1,2,0:T(8,128)(2,1)} copy(bf16[1,128,512]{2,1,0:T(8,128)(2,1)S(1)} %copy-done.6) | data formatting | bytes 262144 | tf_op args[2]
  22.3 0.6 pad_clamp_fusion.1
  22.9 0.7 %copy.101 = f32[128,32]{0,1:T(8,128)} copy(f32[128,32]{1,0:T(8,128)S(1)} %bitcast.138) | data formatting | bytes 32768 | tf_op jit(solution)/shard_map/while/body/eval_jaxpr/sub | solution.py:41
  23.6 0.3 copy.107
  23.9 0.1 copy.106
  24.0 0.6 pad_clamp_fusion
  24.6 0.1 copy.108
  24.7 0.2 convolution_bitcast_fusion.1
  24.9 0.8 %gather_fusion = f32[32,128,128]{1,2,0:T(8,128)S(1)} fusion(f32[128,128,4]{0,1,2:T(8,128)S(1)} %convolution_bitcast_fusion.1, s32[1024]{0:T(1024)} %pad_clamp_fusion.1), kind=kCustom, calls=%fused_computation.2 | custom fusion | bytes 4194432 | tf_op jit(solution)/shard_map/while/body/eval_jaxpr/jit(_take)/gather | solution.py:34
  25.8 1.4 %multiply_bitcast_fusion = (f32[128,32]{0,1:T(8,128)}, f32[128,32]{0,1:T(8,128)S(1)}) fusion(f32[1,128,32]{1,2,0:T(8,128)} %copy.114, f32[32]{0:T(128)} %slice_bitcast_fusion.4, f32[128]{0:T(128)} %copy-done.17, f32[1,128,32]{1,2,0:T(8,128)} %param.22, f32[32]{0:T(128)} %param.26), kind=kLoop, calls=%fused_computation.72 | loop fusion | flops 40960 | bytes 66304 | tf_op jit(solution)/shard_map/while/body/eval_jaxpr/mul | solution.py:47
  27.2 1.8 %gather_fusion.2 = bf16[32,128,128]{2,1,0:T(8,128)(2,1)} fusion(bf16[128,4,128]{2,0,1:T(8,128)(2,1)S(1)} %bitcast.132, s32[1024]{0:T(1024)} %pad_clamp_fusion), kind=kCustom, calls=%fused_computation.clone | custom fusion | bytes 2097280 | tf_op jit(solution)/shard_map/while/body/eval_jaxpr/jit(_take)/gather | solution.py:36
  29.0 4.0 %fusion.12 = f32[1,128,32,64]{1,3,2,0:T(8,128)S(1)} fusion(bf16[128,32,64]{0,2,1:T(8,128)(2,1)} %bitcast.140, f32[32,128,128]{1,2,0:T(8,128)S(1)} %gather_fusion, f32[128,32]{0,1:T(8,128)S(1)} %get-tuple-element.74, f32[128,32]{0,1:T(8,128)S(1)} %copy-done.12, pred[32]{0:T(512)(128)(4,1)S(1)} %copy-done.23, pred[128,128]{0,1:T(8,128)(4,1)S(1)} %copy-done.13), kind=kOutput, calls=%fused_computation.16 | convolution fusion | flops 405798912 | bytes 3719200 | tf_op jit(solution)/shard_map/while/body/eval_jaxpr/cijh,cjhp->cihp/dot_general | solution.py:44
  33.0 2.2 %fusion.17 = f32[1,128,32,64]{1,3,2,0:T(8,128)S(1)} fusion(f32[1,128,32,64]{1,3,2,0:T(8,128)S(1)} %fusion.12, f32[128,32,64]{0,2,1:T(8,128)S(1)} %bitcast.134, bf16[32,128,128]{2,1,0:T(8,128)(2,1)S(1)} %copy-done, f32[1,128,32,64]{1,3,2,0:T(8,128)S(1)} %bitcast.135, pred[32]{0:T(512)(128)(4,1)S(1)} %copy-done.23, f32[32]{0:T(128)S(1)} %copy-done.22, ...), kind=kOutput, calls=%fused_computation.20 | convolution fusion | flops 404226048 | bytes 5259424 | tf_op jit(solution)/shard_map/while/body/eval_jaxpr/cihn,cnhp->cihp/dot_general | solution.py:61
  35.3 0.3 copy.110
  35.7 0.3 copy-done.19
  36.0 0.1 mul.246
  36.1 0.1 mul.247
  36.2 0.1 copy-done.7
  36.2 0.1 copy.113
  36.4 1.8 %gather_fusion.3 = bf16[32,128,128]{2,1,0:T(8,128)(2,1)} fusion(bf16[128,4,128]{2,0,1:T(8,128)(2,1)S(1)} %bitcast.133, s32[1024]{0:T(1024)} %pad_clamp_fusion), kind=kCustom, calls=%fused_computation.1.clone | custom fusion | bytes 2097280 | tf_op jit(solution)/shard_map/while/body/eval_jaxpr/jit(_take)/gather | solution.py:35
  38.1 0.4 multiply_reduce_fusion
  38.6 2.7 %fusion = f32[32,128,64]{1,2,0:T(8,128)S(1)} fusion(bf16[128,32,64]{0,2,1:T(8,128)(2,1)S(1)} %bitcast.141, bf16[32,128,128]{2,1,0:T(8,128)(2,1)} %gather_fusion.3, f32[128,32]{0,1:T(8,128)S(1)} %copy-done.15, pred[32]{0:T(512)(128)(4,1)S(1)} %copy-done.24), kind=kOutput, calls=%fused_computation.4 | convolution fusion | flops 404226048 | bytes 2637856 | tf_op jit(solution)/shard_map/while/body/eval_jaxpr/cjhn,cjhp->cnhp/dot_general | solution.py:46
  41.4 0.4 fusion.26
  41.8 0.1 fusion.51
  41.9 0.7 %reshape.503 = bf16[4,1,1,512]{3,2,1,0:T(2,128)(2,1)S(1)} reshape(bf16[4,2,256]{2,1,0:T(2,128)(2,1)} %all-to-all-done) | data formatting | bytes 8192
  42.6 0.7 %gather_fusion.1 = bf16[32,4,128]{2,1,0:T(4,128)(2,1)S(1)} fusion(bf16[4,4,128]{2,0,1:T(4,128)(2,1)S(1)} %bitcast.144, s32[1024]{0:T(1024)} %pad_clamp_fusion.1), kind=kCustom, calls=%fused_computation.3 | custom fusion | bytes 65664 | tf_op jit(solution)/shard_map/jit(_take)/gather | solution.py:80
  43.3 0.4 fusion.18
  43.8 0.1 convert_element_type.108
  43.9 0.8 %reduce.6 = bf16[4,2048]{1,0:T(4,128)(2,1)S(1)} reduce(bf16[4,1,2048]{2,1,0:T(2,128)(2,1)S(1)} %convert_element_type.108, bf16[]{:T(256)} %broadcast.360), dimensions={1}, to_apply=%convert_element_type.108.reduce_sub_computation | reduce | bytes 32770 | tf_op jit(solution)/shard_map/convert_element_type | solution.py:138
  44.6 0.6 reshape.504
  45.3 5.1 %all-to-all-start.1 = ((bf16[4,2,1024]{2,1,0:T(2,128)(2,1)}), bf16[4,2,1024]{2,1,0:T(2,128)(2,1)S(1)}, u32[]{:S(2)}, u32[]{:S(2)}) async-start(bf16[4,2,1024]{2,1,0:T(2,128)(2,1)} %reshape.504), calls=%async_computation.1 | async-start | bytes 32768 | tf_op jit(solution)/shard_map/all_to_all | solution.py:137
  50.3 0.2 fusion.21
  50.5 1.0 %copy.120 = bf16[1,128,2048]{2,1,0:T(8,128)(2,1)} copy(bf16[1,128,2048]{1,2,0:T(8,128)(2,1)S(1)} %fusion.26) | data formatting | bytes 1048576
  51.6 0.1 mul.262
  51.6 0.1 mul.263
  51.8 0.1 mul.257
  51.8 0.1 mul.258
  51.9 4.0 %all-to-all-done.1 = bf16[4,2,1024]{2,1,0:T(2,128)(2,1)S(1)} async-done(((bf16[4,2,1024]{2,1,0:T(2,128)(2,1)}), bf16[4,2,1024]{2,1,0:T(2,128)(2,1)S(1)}, u32[]{:S(2)}, u32[]{:S(2)}) %all-to-all-start.1) | async-done | bytes 16416 | tf_op jit(solution)/shard_map/all_to_all | solution.py:137
  56.0 0.2 multiply_reduce_fusion.1
  56.2 5.6 %all-reduce = (f32[1,128]{1,0:T(1,128)S(1)}, f32[1,4]{1,0:T(1,128)S(1)}) all-reduce(f32[1,128]{1,0:T(1,128)S(1)} %bitcast.145, f32[1,4]{1,0:T(1,128)S(1)} %bitcast.146), channel_id=1, replica_groups=mesh['rep'=2,'sample'=4,'head'=4] {'head'}, use_global_device_ids=true, to_apply=%region_2.4 | all-reduce | flops 132 | bytes 1056 | tf_op jit(solution)/shard_map/psum | solution.py:120
  61.9 1.2 %multiply_convert_fusion = bf16[1,128,2048]{2,1,0:T(8,128)(2,1)} fusion(f32[128]{0:T(128)S(1)} %copy-done.18, f32[2048]{0:T(1024)S(1)} %copy-done.9, f32[128]{0:T(128)S(1)} %rsqrt_bitcast_fusion.1, f32[1,128,2048]{2,1,0:T(8,128)S(1)} %copy.110, bf16[1,128,2048]{2,1,0:T(8,128)(2,1)S(1)} %copy-done.3), kind=kLoop, calls=%fused_computation.41 | loop fusion | flops 2621440 | bytes 2106368 | tf_op jit(solution)/shard_map/convert_element_type | solution.py:122
  63.1 0.1 multiply_convert_fusion.1
  63.2 0.6 copy.121
  (63 shorter events, 0.3 us)
Async XLA Ops:
  0.6 19.7 %copy-start.8 = (bf16[1,4,512]{2,1,0:T(4,128)(2,1)S(1)}, bf16[1,4,512]{2,1,0:T(4,128)(2,1)}, u32[]{:S(2)}) copy-start(bf16[1,4,512]{2,1,0:T(4,128)(2,1)} %param.32) | copy-start | bytes 12292
  0.6 18.5 %copy-start.2 = (bf16[1,128,2048]{2,1,0:T(8,128)(2,1)S(1)}, bf16[1,128,2048]{2,1,0:T(8,128)(2,1)}, u32[]{:S(2)}) copy-start(bf16[1,128,2048]{2,1,0:T(8,128)(2,1)} %param.18) | copy-start | bytes 1572868
  0.7 20.8 %copy-start.6 = (bf16[1,128,512]{2,1,0:T(8,128)(2,1)S(1)}, bf16[1,128,512]{2,1,0:T(8,128)(2,1)}, u32[]{:S(2)}) copy-start(bf16[1,128,512]{2,1,0:T(8,128)(2,1)} %param.20) | copy-start | bytes 393220
  3.5 38.4 %all-to-all-start = ((bf16[4,2,256]{2,1,0:T(2,128)(2,1)}), bf16[4,2,256]{2,1,0:T(2,128)(2,1)}, u32[]{:S(2)}, u32[]{:S(2)}) async-start(bf16[4,2,256]{2,1,0:T(2,128)(2,1)} %reshape.502), calls=%async_computation | async-start | bytes 8192 | tf_op jit(solution)/shard_map/all_to_all | solution.py:129
  10.5 0.5 copy-start.17
  11.8 11.8 %copy-start.4 = (f32[1,128,2048]{2,1,0:T(8,128)S(1)}, f32[1,128,2048]{2,1,0:T(8,128)}, u32[]{:S(2)}) copy-start(f32[1,128,2048]{2,1,0:T(8,128)} %param.24) | copy-start | bytes 3145732
  25.7 3.3 %copy-start.12 = (f32[128,32]{0,1:T(8,128)S(1)}, f32[128,32]{0,1:T(8,128)}, u32[]{:S(2)}) copy-start(f32[128,32]{0,1:T(8,128)} %copy.101) | copy-start | bytes 49156
  25.7 3.3 %copy-start.13 = (pred[128,128]{0,1:T(8,128)(4,1)S(1)}, pred[128,128]{0,1:T(8,128)(4,1)}, u32[]{:S(2)}) copy-start(pred[128,128]{0,1:T(8,128)(4,1)} %iota_compare_fusion) | copy-start | bytes 49156
  25.7 3.3 %copy-start.23 = (pred[32]{0:T(512)(128)(4,1)S(1)}, pred[32]{0:T(512)(128)(4,1)}, u32[]{:S(2)}) copy-start(pred[32]{0:T(512)(128)(4,1)} %compare_and_fusion) | copy-start | bytes 100
  29.0 4.0 %copy-start = (bf16[32,128,128]{2,1,0:T(8,128)(2,1)S(1)}, bf16[32,128,128]{2,1,0:T(8,128)(2,1)}, u32[]{:S(2)}) copy-start(bf16[32,128,128]{2,1,0:T(8,128)(2,1)} %gather_fusion.2) | copy-start | bytes 3145732
  29.0 4.0 %copy-start.1 = (f32[1,128,2048]{1,2,0:T(8,128)S(1)}, f32[1,128,2048]{1,2,0:T(8,128)}, u32[]{:S(2)}) copy-start(f32[1,128,2048]{1,2,0:T(8,128)} %copy.109) | copy-start | bytes 3145732
  29.0 4.0 %copy-start.22 = (f32[32]{0:T(128)S(1)}, f32[32]{0:T(128)}, u32[]{:S(2)}) copy-start(f32[32]{0:T(128)} %param.27) | copy-start | bytes 388
  35.3 0.7 %copy-start.19 = (bf16[1,4,512]{2,1,0:T(4,128)(2,1)S(1)}, bf16[1,4,512]{2,1,0:T(4,128)(2,1)}, u32[]{:S(2)}) copy-start(bf16[1,4,512]{2,1,0:T(4,128)(2,1)} %param.31) | copy-start | bytes 12292
  35.3 0.7 %copy-start.16 = (f32[32]{0:T(128)S(1)}, f32[32]{0:T(128)}, u32[]{:S(2)}) copy-start(f32[32]{0:T(128)} %param.26) | copy-start | bytes 388
  35.3 0.7 %copy-start.20 = (f32[32]{0:T(128)S(1)}, f32[32]{0:T(128)}, u32[]{:S(2)}) copy-start(f32[32]{0:T(128)} %param.25) | copy-start | bytes 388
  35.3 0.7 %copy-start.21 = (f32[1,4,32]{2,1,0:T(4,128)S(1)}, f32[1,4,32]{2,1,0:T(4,128)}, u32[]{:S(2)}) copy-start(f32[1,4,32]{2,1,0:T(4,128)} %param.33) | copy-start | bytes 1540
  35.3 0.7 %copy-start.25 = (f32[32]{0:T(128)S(1)}, f32[32]{0:T(128)}, u32[]{:S(2)}) copy-start(f32[32]{0:T(128)} %fusion.59) | copy-start | bytes 388
  35.3 0.9 %copy-start.7 = (bf16[1,128,512]{1,2,0:T(8,128)(2,1)S(1)}, bf16[1,128,512]{1,2,0:T(8,128)(2,1)}, u32[]{:S(2)}) copy-start(bf16[1,128,512]{1,2,0:T(8,128)(2,1)} %copy.112) | copy-start | bytes 393220
  35.9 2.2 %copy-start.3 = (bf16[1,128,2048]{2,1,0:T(8,128)(2,1)S(1)}, bf16[1,128,2048]{2,1,0:T(8,128)(2,1)}, u32[]{:S(2)}) copy-start(bf16[1,128,2048]{2,1,0:T(8,128)(2,1)} %param.19) | copy-start | bytes 1572868
  35.9 2.6 %copy-start.5 = (bf16[1,128,2048]{1,2,0:T(8,128)(2,1)S(1)}, bf16[1,128,2048]{1,2,0:T(8,128)(2,1)}, u32[]{:S(2)}) copy-start(bf16[1,128,2048]{1,2,0:T(8,128)(2,1)} %copy.103) | copy-start | bytes 1572868
  36.0 2.6 %copy-start.15 = (f32[128,32]{0,1:T(8,128)S(1)}, f32[128,32]{0,1:T(8,128)}, u32[]{:S(2)}) copy-start(f32[128,32]{0,1:T(8,128)} %get-tuple-element.73) | copy-start | bytes 49156
  36.0 2.6 %copy-start.24 = (pred[32]{0:T(512)(128)(4,1)S(1)}, pred[32]{0:T(512)(128)(4,1)}, u32[]{:S(2)}) copy-start(pred[32]{0:T(512)(128)(4,1)} %compare_and_fusion) | copy-start | bytes 100
  38.6 3.2 %copy-start.14 = (bf16[4,4,128]{2,1,0:T(4,128)(2,1)S(1)}, bf16[4,4,128]{2,1,0:T(4,128)(2,1)}, u32[]{:S(2)}) copy-start(bf16[4,4,128]{2,1,0:T(4,128)(2,1)} %reshape.441) | copy-start | bytes 12292
  41.3 9.0 %copy-start.26 = (s32[32]{0:T(128)S(1)}, s32[32]{0:T(128)}, u32[]{:S(2)}) copy-start(s32[32]{0:T(128)} %get-tuple-element.80) | copy-start | bytes 388
  41.3 14.6 %copy-start.10 = (bf16[1,4,2048]{2,1,0:T(4,128)(2,1)S(1)}, bf16[1,4,2048]{2,1,0:T(4,128)(2,1)}, u32[]{:S(2)}) copy-start(bf16[1,4,2048]{2,1,0:T(4,128)(2,1)} %param.30) | copy-start | bytes 49156
  41.4 14.6 %copy-start.11 = (bf16[1,4,2048]{2,1,0:T(4,128)(2,1)S(1)}, bf16[1,4,2048]{2,1,0:T(4,128)(2,1)}, u32[]{:S(2)}) copy-start(bf16[1,4,2048]{2,1,0:T(4,128)(2,1)} %param.29) | copy-start | bytes 49156
  41.4 20.5 %copy-start.9 = (f32[2048]{0:T(1024)S(1)}, f32[2048]{0:T(1024)}, u32[]{:S(2)}) copy-start(f32[2048]{0:T(1024)} %param.28) | copy-start | bytes 24580
  41.4 20.5 %copy-start.18 = (f32[128]{0:T(128)S(1)}, f32[128]{0:T(128)}, u32[]{:S(2)}) copy-start(f32[128]{0:T(128)} %copy-done.17) | copy-start | bytes 1540
  45.3 10.7 %all-to-all-start.1 = ((bf16[4,2,1024]{2,1,0:T(2,128)(2,1)}), bf16[4,2,1024]{2,1,0:T(2,128)(2,1)S(1)}, u32[]{:S(2)}, u32[]{:S(2)}) async-start(bf16[4,2,1024]{2,1,0:T(2,128)(2,1)} %reshape.504), calls=%async_computation.1 | async-start | bytes 32768 | tf_op jit(solution)/shard_map/all_to_all | solution.py:137
